TPU v7x, 128 devices: a whole 4x4x4 slice. The times are simulated.
128 devices in a mesh: row: 16 (over y, x), col: 8 (over z, core).
Axes of the slice: x: 4, y: 4, z: 4, core: 2. Of those that a mesh axis runs over, the one named last changes fastest.
Arguments:
- features: bfloat16 [32768, 256], P(('row', 'col')), may hold values from -6 to 6
- out_degree: int32 [32768], P('row'), may hold values from 8 to 1024
- in_degree: int32 [32768], P('col'), may hold values from 8 to 1024
- tile_blocks: int32 [16, 8, 2, 128], P('row', 'col'), may hold values from 0 to 31, as said below
- tile_count: int32 [16, 8], P('row', 'col'), may hold values from 16 to 128, as said below
- tile_weights: bfloat16 [16, 8, 128, 128, 128], P('row', 'col'), may hold values from 0 to 4, as said below
- weight: bfloat16 [256, 256], replicated, may hold values from -0.375 to 0.375
- cotangent: bfloat16 [32768, 256], P(('col', 'row')), may hold values from -6 to 6
Outputs:
- hidden: bfloat16 [32768, 256], P(('col', 'row'))
- input_grad: bfloat16 [32768, 256], P(('row', 'col'))
- weight_grad: float32 [256, 256], replicated
Inputs may be any that keep to these rules, and one draw needn't show every extreme that they name: `tile_blocks`: entry [r, c, 0, s] is a target block below 32, entry [r, c, 1, s] a source block below 16; the pairs of one device position are distinct. `tile_count`: live tile slots of a device position are its first ones; some position has exactly 128. `tile_weights`: Non-negative edge weights.
All inputs are finite; a program needn't handle non-finite values.
Results may differ from a plain program's by a relative error of at most 0.0067.
Values may be sent and summed in bfloat16 or wider, within the bound.
No kernel may reach another device: no remote copies, remote signals or barrier semaphores. Data moves between devices by JAX's collectives and lax.ppermute only.
A program may use at most 192 MiB of HBM per device.

v0:
```python
import jax
import jax.numpy as jnp
from jax import lax
from jax.sharding import PartitionSpec as P

TILE = 128


def silu_slope(pre_act):
    gate_sig = jax.nn.sigmoid(pre_act)
    return gate_sig * (1.0 + pre_act * (1.0 - gate_sig))


def tile_sum(tile_vals, dst_ids, src_ids, live_count, inputs, dst_blocks, transpose):
    feat_width = inputs.shape[1]
    group_size = min(128, tile_vals.shape[0])
    block_stack = inputs.reshape(-1, TILE, feat_width)
    group_count = (live_count + group_size - 1) // group_size

    def add_group(group_at, running):
        first_slot = group_at * group_size
        picked = jnp.take(block_stack, src_ids, axis=0)
        if transpose:
            products = jnp.einsum(
                "trc,trh->tch", tile_vals, picked, preferred_element_type=jnp.float32
            )
        else:
            products = jnp.einsum(
                "trc,tch->trh", tile_vals, picked, preferred_element_type=jnp.float32
            )
        slot_ids = first_slot + jnp.arange(group_size)
        is_live = slot_ids < live_count
        masked = jnp.where(is_live[:, None], products.reshape(group_size, -1), 0.0)
        return running.at[dst_ids].add(masked)

    start_sum = jnp.zeros((dst_blocks, TILE * feat_width), jnp.float32)
    running = lax.fori_loop(0, group_count, add_group, start_sum)
    return running.reshape(dst_blocks * TILE, feat_width)


def shards(
    features, out_degree, in_degree, tile_blocks, tile_count, tile_weights, weight, cotangent
):
    row_count = features.shape[0]
    row_at = lax.axis_index("row")
    col_at = lax.axis_index("col")
    out_strip = lax.rsqrt(out_degree.astype(jnp.float32))
    in_strip = lax.rsqrt(in_degree.astype(jnp.float32))
    own_out = lax.dynamic_slice_in_dim(out_strip, col_at * row_count, row_count, 0)
    src_scaled = (features.astype(jnp.float32) * own_out[:, None]).astype(jnp.bfloat16)
    source = lax.all_gather(src_scaled, "col", axis=0, tiled=True)
    blocks = tile_blocks[0, 0]
    live_count = tile_count[0, 0]
    tile_vals = tile_weights[0, 0]
    partial_value = tile_sum(
        tile_vals, blocks[0], blocks[1], live_count, source, in_strip.shape[0] // TILE, False
    )
    contract_rows = (((0,), (0,)), ((), ()))
    summed = lax.psum(partial_value, "row")
    agg_strip = (summed * in_strip[:, None]).astype(jnp.bfloat16)
    pre_strip = jnp.dot(agg_strip, weight, preferred_element_type=jnp.float32)
    strip_grads = lax.all_gather(cotangent, "row", axis=0, tiled=True)
    grad_strip = (strip_grads.astype(jnp.float32) * silu_slope(pre_strip)).astype(jnp.bfloat16)
    own_pre = lax.dynamic_slice_in_dim(pre_strip, row_at * row_count, row_count, 0)
    hidden = jax.nn.silu(own_pre).astype(jnp.bfloat16)
    agg_rows = lax.dynamic_slice_in_dim(agg_strip, row_at * row_count, row_count, 0)
    pre_grad = lax.dynamic_slice_in_dim(grad_strip, row_at * row_count, row_count, 0)
    weight_part = lax.dot_general(
        agg_rows, pre_grad, contract_rows, preferred_element_type=jnp.float32
    )
    back_rows = jnp.dot(grad_strip, weight.T, preferred_element_type=jnp.float32)
    target_grad = (back_rows * in_strip[:, None]).astype(jnp.bfloat16)
    weight_grad = lax.psum(weight_part, ("row", "col"))
    back_part = tile_sum(
        tile_vals, blocks[1], blocks[0], live_count, target_grad, source.shape[0] // TILE, True
    )
    src_sum = lax.psum_scatter(back_part, "col", scatter_dimension=0, tiled=True)
    input_grad = (src_sum * own_out[:, None]).astype(jnp.bfloat16)
    return (hidden, input_grad, weight_grad)


def solution(mesh):
    placed = (
        P(("row", "col"), None),
        P("row"),
        P("col"),
        P("row", "col", None, None),
        P("row", "col"),
        P("row", "col", None, None, None),
        P(),
        P(("col", "row"), None),
    )
    return jax.shard_map(
        shards,
        mesh=mesh,
        in_specs=placed,
        out_specs=(P(("col", "row"), None), P(("row", "col"), None), P()),
        check_vma=False,
    )
```

profile of v0, /device:TPU:1, one launch (start us, length us, event | category | flops | bytes accessed | tf_op | source)
XLA Modules:
  0.0 580.1 jit_solution(587805703968408114)
XLA Ops:
  7.2 0.8 fusion.16
  8.5 1.7 multiply_convert_fusion.4
  10.9 0.8 slice_bitcast_fusion
  11.7 25.7 %all-gather.3.cloned.1.call-done = bf16[2048,256]{1,0:T(8,128)(2,1)} async-done(((bf16[256,256]{1,0:T(8,128)(2,1)}), bf16[2048,256]{1,0:T(8,128)(2,1)}) %all-gather.3.cloned.1.call-update) | async-done | bytes 1048592 | tf_op jit(solution)/shard_map/all_gather | solution.py:51
  37.4 2.3 broadcast_in_dim.54
  39.7 94.9 %while.20 = (s32[]{:T(128)}, f32[32,32768]{1,0:T(8,128)}, s32[]{:T(128)}, s32[128]{0:T(128)S(1)}, s32[]{:T(128)}, /*index=5*/s32[128]{0:T(128)S(1)}, bf16[16,128...) while((s32[]{:T(128)}, f32[32,32768]{1,0:T(8,128)}, s32[]{:T(128)}, ...), condition=%wide.region_2.3_spmd, body=%wide.region_0.2_spmd.sunk | while | flops 1086327552 | bytes 197141120 | solution.py:37
  39.8 6.6 %gather_fusion = bf16[128,128,256]{2,1,0:T(8,128)(2,1)} fusion(bf16[16,128,256]{2,1,0:T(8,128)(2,1)S(1)} %get-tuple-element.277, s32[1024]{0:T(1024)S(1)} %pad_clamp_fusion.4), kind=kCustom, calls=%fused_computation.clone.1 | custom fusion | bytes 16777728 | tf_op jit(solution)/shard_map/while/body/jit(_take)/gather | solution.py:22
  47.0 13.2 %convolution_bitcast_fusion.4 = f32[128,128,256]{1,2,0:T(8,128)} fusion(bf16[128,128,128]{2,1,0:T(8,128)(2,1)} %get-tuple-element.278, bf16[128,128,256]{2,1,0:T(8,128)(2,1)} %gather_fusion, pred[128]{0:T(512)(128)(4,1)S(1)} %get-tuple-element.237), kind=kOutput, calls=%fused_computation.5.clone.1 | convolution fusion | flops 1077936128 | bytes 29360256 | tf_op jit(solution)/shard_map/while/body/trc,tch->trh/dot_general | solution.py:28
  60.2 17.7 %copy.29 = f32[128,128,256]{0,2,1:T(8,128)} copy(f32[128,128,256]{1,2,0:T(8,128)} %convolution_bitcast_fusion.4) | data formatting | bytes 33554432 | tf_op jit(solution)/shard_map/while/body/trc,tch->trh/dot_general | solution.py:28
  77.9 11.2 %bitcast_select_fusion.4 = f32[128,32768]{0,1:T(8,128)} fusion(f32[128,128,256]{0,2,1:T(8,128)} %copy.29, pred[128]{0:T(512)(128)(4,1)S(1)} %get-tuple-element.238), kind=kLoop, calls=%fused_computation.4.clone.1 | loop fusion | flops 4194304 | bytes 33554560 | tf_op jit(solution)/shard_map/while/body/jit(_where)/select_n | solution.py:33
  89.1 17.4 %copy.30 = f32[128,32768]{1,0:T(8,128)} copy(f32[128,32768]{0,1:T(8,128)} %bitcast_select_fusion.4) | data formatting | bytes 33554432 | tf_op jit(solution)/shard_map/while/body/jit(_where)/select_n | solution.py:33
  106.6 27.7 %scatter_fusion = f32[32,32768]{1,0:T(8,128)} fusion(f32[32,32768]{1,0:T(8,128)} %get-tuple-element.262, s32[128]{0:T(128)S(1)} %get-tuple-element.235, f32[128,32768]{1,0:T(8,128)} %copy.30), kind=kCustom, calls=%fused_computation.2.clone.1 | custom fusion | flops 4194304 | bytes 50332160 | tf_op jit(solution)/shard_map/while/body/scatter-add | solution.py:34
  134.6 4.9 reshape.111
  140.4 101.8 %all-reduce.3.cloned.1.call-done = f32[4096,256]{1,0:T(8,128)} async-done(((f32[4096,256]{1,0:T(8,128)}), f32[4096,256]{1,0:T(8,128)}) %all-reduce.3.cloned.1.call-update) | async-done | bytes 4194320 | tf_op jit(solution)/shard_map/psum | solution.py:59
  242.2 2.6 multiply_convert_fusion.1
  244.7 42.9 %all-gather.5.cloned.1.call-done = bf16[4096,256]{1,0:T(8,128)(2,1)} async-done(((bf16[256,256]{1,0:T(8,128)(2,1)}), bf16[4096,256]{1,0:T(8,128)(2,1)}) %all-gather.5.cloned.1.call-update) | async-done | bytes 2097168 | tf_op jit(solution)/shard_map/all_gather | solution.py:62
  287.7 5.2 multiply_convert_fusion
  292.9 2.0 fusion.12
  295.0 92.8 %while.21 = (s32[]{:T(128)}, f32[16,32768]{1,0:T(8,128)S(1)}, s32[]{:T(128)}, s32[128]{0:T(128)S(1)}, s32[]{:T(128)}, /*index=5*/s32[128]{0:T(128)S(1)}, bf16[32...) while((s32[]{:T(128)}, f32[16,32768]{1,0:T(8,128)S(1)}, s32[]{:T(128)}, ...), condition=%wide.region_6.7_spmd, body=%wide.region_4.6_spmd.sunk | while | flops 1086327552 | bytes 197141120 | solution.py:37
  295.3 8.2 %gather_fusion.1 = bf16[128,128,256]{2,1,0:T(8,128)(2,1)} fusion(bf16[32,128,256]{2,1,0:T(8,128)(2,1)} %get-tuple-element.307, s32[1024]{0:T(1024)S(1)} %pad_clamp_fusion.5), kind=kCustom, calls=%fused_computation.1.clone.1 | custom fusion | bytes 16777728 | tf_op jit(solution)/shard_map/while/body/jit(_take)/gather | solution.py:22
  304.1 12.8 %convolution_bitcast_fusion.5 = f32[128,128,256]{1,2,0:T(8,128)} fusion(bf16[128,128,128]{2,1,0:T(8,128)(2,1)} %get-tuple-element.308, bf16[128,128,256]{2,1,0:T(8,128)(2,1)} %gather_fusion.1, pred[128]{0:T(512)(128)(4,1)S(1)} %get-tuple-element.249), kind=kOutput, calls=%fused_computation.19.clone.1 | convolution fusion | flops 1077936128 | bytes 29360256 | tf_op jit(solution)/shard_map/while/body/trc,trh->tch/dot_general | solution.py:24
  316.9 17.7 %copy.31 = f32[128,128,256]{0,2,1:T(8,128)} copy(f32[128,128,256]{1,2,0:T(8,128)} %convolution_bitcast_fusion.5) | data formatting | bytes 33554432 | tf_op jit(solution)/shard_map/while/body/trc,trh->tch/dot_general | solution.py:24
  334.6 11.3 %bitcast_select_fusion.5 = f32[128,32768]{0,1:T(8,128)} fusion(f32[128,128,256]{0,2,1:T(8,128)} %copy.31, pred[128]{0:T(512)(128)(4,1)S(1)} %get-tuple-element.250), kind=kLoop, calls=%fused_computation.18.clone.1 | loop fusion | flops 4194304 | bytes 33554560 | tf_op jit(solution)/shard_map/while/body/jit(_where)/select_n | solution.py:33
  345.9 17.4 %copy.32 = f32[128,32768]{1,0:T(8,128)} copy(f32[128,32768]{0,1:T(8,128)} %bitcast_select_fusion.5) | data formatting | bytes 33554432 | tf_op jit(solution)/shard_map/while/body/jit(_where)/select_n | solution.py:33
  363.3 24.3 %scatter_fusion.1 = f32[16,32768]{1,0:T(8,128)S(1)} fusion(f32[16,32768]{1,0:T(8,128)S(1)} %get-tuple-element.292, s32[128]{0:T(128)S(1)} %get-tuple-element.247, f32[128,32768]{1,0:T(8,128)} %copy.32), kind=kCustom, calls=%fused_computation.3.clone.1 | custom fusion | flops 4194304 | bytes 50332160 | tf_op jit(solution)/shard_map/while/body/scatter-add | solution.py:34
  387.9 1.5 reshape.113
  389.5 1.7 multiply_convert_fusion.3
  391.2 1.9 fusion.13
  393.1 28.5 %reduce-scatter.2.cloned.1.call-done = f32[256,256]{1,0:T(8,128)} async-done(((f32[2048,256]{1,0:T(8,128)}), f32[256,256]{1,0:T(8,128)}) %reduce-scatter.2.cloned.1.call-update) | async-done | bytes 262160 | tf_op jit(solution)/shard_map/reduce_scatter | solution.py:77
  421.5 1.7 multiply_convert_fusion.2
  423.3 148.3 %all-reduce.5.cloned.1.call-done = f32[256,256]{1,0:T(8,128)} async-done(((f32[256,256]{1,0:T(8,128)}), f32[256,256]{1,0:T(8,128)}) %all-reduce.5.cloned.1.call-update) | async-done | bytes 262160 | tf_op jit(solution)/shard_map/psum | solution.py:73
  571.6 1.7 copy.50
  (34 shorter events, 3.0 us)
Async XLA Ops:
  7.2 280.5 %copy-start = (bf16[256,256]{1,0:T(8,128)(2,1)S(1)}, bf16[256,256]{1,0:T(8,128)(2,1)}, u32[]{:S(2)}) copy-start(bf16[256,256]{1,0:T(8,128)(2,1)} %param.18) | copy-start | bytes 393220
  7.2 30.2 %all-gather.3.cloned.1.call-start = ((), (), s32[]{:S(2)}) async-start(), calls=%async_computation.1 | async-start | bytes 1179648 | tf_op jit(solution)/shard_map/all_gather | solution.py:51
  8.0 0.5 copy-start.6
  10.2 231.9 %all-reduce.3.cloned.1.call-start = ((), (), s32[]{:S(2)}) async-start(), calls=%async_computation.2 | async-start | bytes 8388608 | tf_op jit(solution)/shard_map/psum | solution.py:59
  37.4 2.3 copy-start.2
  139.5 0.8 copy-start.5
  139.5 148.1 %all-gather.5.cloned.1.call-start = ((), (), s32[]{:S(2)}) async-start(), calls=%async_computation.3 | async-start | bytes 2228224 | tf_op jit(solution)/shard_map/all_gather | solution.py:62
  140.3 281.3 %reduce-scatter.2.cloned.1.call-start = ((), (), s32[]{:S(2)}) async-start(), calls=%async_computation.4 | async-start | bytes 2359296 | tf_op jit(solution)/shard_map/reduce_scatter | solution.py:77
  244.7 48.1 %copy-start.3 = (bf16[4096,256]{1,0:T(8,128)(2,1)}, bf16[4096,256]{1,0:T(8,128)(2,1)S(1)}, u32[]{:S(2)}) copy-start(bf16[4096,256]{1,0:T(8,128)(2,1)S(1)} %multiply_convert_fusion.1) | copy-start | bytes 6291460
  292.9 2.0 copy-start.4
  387.9 33.7 %copy-start.7 = (f32[256]{0:T(256)S(1)}, f32[256]{0:T(256)}, u32[]{:S(2)}) copy-start(f32[256]{0:T(256)} %copy-done.6) | copy-start | bytes 3076
  387.9 185.4 %copy-start.1 = (bf16[256,256]{1,0:T(8,128)(2,1)S(1)}, bf16[256,256]{1,0:T(8,128)(2,1)}, u32[]{:S(2)}) copy-start(bf16[256,256]{1,0:T(8,128)(2,1)} %param.18) | copy-start | bytes 393220
  389.4 182.2 %all-reduce.5.cloned.1.call-start = ((), (), s32[]{:S(2)}) async-start(), calls=%async_computation.5 | async-start | bytes 524288 | tf_op jit(solution)/shard_map/psum | solution.py:73
Sparse Core Ops, SparseCore 0:
  10.3 27.0 all-gather.2
  139.7 102.4 all-reduce.2
  244.3 43.3 all-gather.4
  389.5 31.9 reduce-scatter.1
  426.7 144.8 all-reduce.4
where the time goes:
time: 582 us; the launch traced here: 580 us
  waiting for transfers between devices  348 us (60%)
  local copies, waits for them, and re-layouts  96.8 us (17%)
  other arithmetic  84.3 us (14%)
  matrix products  35.2 us (6%)
  between operations  14.8 us (3%)
    psum x1, waiting for transfers between devices, shards(): weight_grad = lax.psum(weight_part, ('row', 'col'))  148 us
    psum x1, waiting for transfers between devices, shards(): summed = lax.psum(partial_value, 'row')  102 us
    scatter-add x2, other arithmetic, add_group(): return running.at[dst_ids].add(masked)  52 us
    all_gather x1, waiting for transfers between devices, shards(): strip_grads = lax.all_gather(cotangent, 'row', axis=0, tiled=True)  42.9 us
    select_n x2, local copies, waits for them, and re-layouts, add_group(): masked = jnp.where(is_live[:, None], products.reshape(group_size, -1), 0.0)  34.9 us
    reduce_scatter x1, waiting for transfers between devices, shards(): lax.psum_scatter(back_part, 'col', scatter_dimension=0, tiled=True)  28.5 us
    all_gather x1, waiting for transfers between devices, shards(): source = lax.all_gather(src_scaled, 'col', axis=0, tiled=True)  25.7 us
    select_n x2, other arithmetic, add_group(): masked = jnp.where(is_live[:, None], products.reshape(group_size, -1), 0.0)  22.5 us
  transfers between devices with their start and end apart: 5, of which 5 were waited for; matrix products, arithmetic and copies ran while one was open for 1% of the time, Pallas kernels for 0%

commit v1 on v0

--- a/solution.py
+++ b/solution.py
@@ -70,7 +70,9 @@
     )
     back_rows = jnp.dot(grad_strip, weight.T, preferred_element_type=jnp.float32)
     target_grad = (back_rows * in_strip[:, None]).astype(jnp.bfloat16)
-    weight_grad = lax.psum(weight_part, ("row", "col"))
+    weight_grad = weight_part
+    for hop_no in ("col", "row"):
+        weight_grad = lax.psum(weight_grad, axis_name=hop_no)
     back_part = tile_sum(
         tile_vals, blocks[1], blocks[0], live_count, target_grad, source.shape[0] // TILE, True
     )

time: 582 us -> 522 us (0.90)
  waiting for transfers between devices: 348 us -> 287 us
    psum x1 -> x2, waiting for transfers between devices: 148 us -> 85.8 us  [shards(): weight_grad = lax.psum(weight_grad, axis_name=hop_no)]
  transfers between devices with their start and end apart: 5 -> 6, of which waited for: 5 -> 5; matrix products, arithmetic and copies ran while one was open for 1% -> 19% of each run, Pallas kernels for 0% -> 0%
where the time goes in v1:
time: 522 us; the launch traced here: 519 us
  waiting for transfers between devices  287 us (55%)
  local copies, waits for them, and re-layouts  96.8 us (19%)
  other arithmetic  84.3 us (16%)
  matrix products  34.2 us (7%)
  between operations  15.2 us (3%)
    psum x1, waiting for transfers between devices, shards(): summed = lax.psum(partial_value, 'row')  102 us
    psum x2, waiting for transfers between devices, shards(): weight_grad = lax.psum(weight_grad, axis_name=hop_no)  85.8 us
    scatter-add x2, other arithmetic, add_group(): return running.at[dst_ids].add(masked)  52 us
    all_gather x1, waiting for transfers between devices, shards(): strip_grads = lax.all_gather(cotangent, 'row', axis=0, tiled=True)  42.9 us
    select_n x2, local copies, waits for them, and re-layouts, add_group(): masked = jnp.where(is_live[:, None], products.reshape(group_size, -1), 0.0)  34.9 us
    reduce_scatter x1, waiting for transfers between devices, shards(): lax.psum_scatter(back_part, 'col', scatter_dimension=0, tiled=True)  29.9 us
    all_gather x1, waiting for transfers between devices, shards(): source = lax.all_gather(src_scaled, 'col', axis=0, tiled=True)  25.7 us
    select_n x2, other arithmetic, add_group(): masked = jnp.where(is_live[:, None], products.reshape(group_size, -1), 0.0)  22.6 us
  transfers between devices with their start and end apart: 6, of which 5 were waited for; matrix products, arithmetic and copies ran while one was open for 19% of the time, Pallas kernels for 0%

profile of v1, /device:TPU:1, one launch (start us, length us, event | category | flops | bytes accessed | tf_op | source)
XLA Modules:
  0.0 518.8 jit_solution(11398628376541662829)
XLA Ops:
  7.2 0.8 fusion.16
  8.6 1.7 multiply_convert_fusion.4
  11.0 0.8 slice_bitcast_fusion
  11.8 25.7 %all-gather.3.cloned.1.call-done = bf16[2048,256]{1,0:T(8,128)(2,1)} async-done(((bf16[256,256]{1,0:T(8,128)(2,1)}), bf16[2048,256]{1,0:T(8,128)(2,1)}) %all-gather.3.cloned.1.call-update) | async-done | bytes 1048592 | tf_op jit(solution)/shard_map/all_gather | solution.py:51
  37.5 2.3 broadcast_in_dim.54
  39.8 94.8 %while.20 = (s32[]{:T(128)}, f32[32,32768]{1,0:T(8,128)}, s32[]{:T(128)}, s32[128]{0:T(128)S(1)}, s32[]{:T(128)}, /*index=5*/s32[128]{0:T(128)S(1)}, bf16[16,128...) while((s32[]{:T(128)}, f32[32,32768]{1,0:T(8,128)}, s32[]{:T(128)}, ...), condition=%wide.region_2.3_spmd, body=%wide.region_0.2_spmd.sunk | while | flops 1086327552 | bytes 197141120 | solution.py:37
  39.8 6.6 %gather_fusion = bf16[128,128,256]{2,1,0:T(8,128)(2,1)} fusion(bf16[16,128,256]{2,1,0:T(8,128)(2,1)S(1)} %get-tuple-element.277, s32[1024]{0:T(1024)S(1)} %pad_clamp_fusion.4), kind=kCustom, calls=%fused_computation.clone.1 | custom fusion | bytes 16777728 | tf_op jit(solution)/shard_map/while/body/jit(_take)/gather | solution.py:22
  47.1 13.2 %convolution_bitcast_fusion.4 = f32[128,128,256]{1,2,0:T(8,128)} fusion(bf16[128,128,128]{2,1,0:T(8,128)(2,1)} %get-tuple-element.278, bf16[128,128,256]{2,1,0:T(8,128)(2,1)} %gather_fusion, pred[128]{0:T(512)(128)(4,1)S(1)} %get-tuple-element.237), kind=kOutput, calls=%fused_computation.5.clone.1 | convolution fusion | flops 1077936128 | bytes 29360256 | tf_op jit(solution)/shard_map/while/body/trc,tch->trh/dot_general | solution.py:28
  60.3 17.6 %copy.29 = f32[128,128,256]{0,2,1:T(8,128)} copy(f32[128,128,256]{1,2,0:T(8,128)} %convolution_bitcast_fusion.4) | data formatting | bytes 33554432 | tf_op jit(solution)/shard_map/while/body/trc,tch->trh/dot_general | solution.py:28
  77.9 11.2 %bitcast_select_fusion.4 = f32[128,32768]{0,1:T(8,128)} fusion(f32[128,128,256]{0,2,1:T(8,128)} %copy.29, pred[128]{0:T(512)(128)(4,1)S(1)} %get-tuple-element.238), kind=kLoop, calls=%fused_computation.4.clone.1 | loop fusion | flops 4194304 | bytes 33554560 | tf_op jit(solution)/shard_map/while/body/jit(_where)/select_n | solution.py:33
  89.1 17.4 %copy.30 = f32[128,32768]{1,0:T(8,128)} copy(f32[128,32768]{0,1:T(8,128)} %bitcast_select_fusion.4) | data formatting | bytes 33554432 | tf_op jit(solution)/shard_map/while/body/jit(_where)/select_n | solution.py:33
  106.6 27.7 %scatter_fusion = f32[32,32768]{1,0:T(8,128)} fusion(f32[32,32768]{1,0:T(8,128)} %get-tuple-element.262, s32[128]{0:T(128)S(1)} %get-tuple-element.235, f32[128,32768]{1,0:T(8,128)} %copy.30), kind=kCustom, calls=%fused_computation.2.clone.1 | custom fusion | flops 4194304 | bytes 50332160 | tf_op jit(solution)/shard_map/while/body/scatter-add | solution.py:34
  134.6 4.9 reshape.111
  140.3 101.8 %all-reduce.4.cloned.1.call-done = f32[4096,256]{1,0:T(8,128)} async-done(((f32[4096,256]{1,0:T(8,128)}), f32[4096,256]{1,0:T(8,128)}) %all-reduce.4.cloned.1.call-update) | async-done | bytes 4194320 | tf_op jit(solution)/shard_map/psum | solution.py:59
  242.1 2.6 multiply_convert_fusion.1
  244.7 42.9 %all-gather.5.cloned.1.call-done = bf16[4096,256]{1,0:T(8,128)(2,1)} async-done(((bf16[256,256]{1,0:T(8,128)(2,1)}), bf16[4096,256]{1,0:T(8,128)(2,1)}) %all-gather.5.cloned.1.call-update) | async-done | bytes 2097168 | tf_op jit(solution)/shard_map/all_gather | solution.py:62
  287.6 5.2 %multiply_convert_fusion = (bf16[4096,256]{1,0:T(8,128)(2,1)S(1)}, f32[4096,256]{1,0:T(8,128)}) fusion(bf16[4096,256]{1,0:T(8,128)(2,1)} %all-gather.5.cloned.1.call-done, bf16[4096,256]{1,0:T(8,128)(2,1)S(1)} %multiply_convert_fusion.1, bf16[256,256]{1,0:T(8,128)(2,1)S(1)} %copy-done), kind=kOutput, calls=%fused_computation.34 | convolution fusion | flops 547356672 | bytes 10616832 | tf_op jit(solution)/shard_map/dot_general | solution.py:61
  292.9 1.9 fusion.12
  294.8 0.9 fusion.13
  296.0 92.9 %while.21 = (s32[]{:T(128)}, f32[16,32768]{1,0:T(8,128)S(1)}, s32[]{:T(128)}, s32[128]{0:T(128)S(1)}, s32[]{:T(128)}, /*index=5*/s32[128]{0:T(128)S(1)}, bf16[32...) while((s32[]{:T(128)}, f32[16,32768]{1,0:T(8,128)S(1)}, s32[]{:T(128)}, ...), condition=%wide.region_6.7_spmd, body=%wide.region_4.6_spmd.sunk | while | flops 1086327552 | bytes 197141120 | solution.py:37
  296.2 8.2 %gather_fusion.1 = bf16[128,128,256]{2,1,0:T(8,128)(2,1)} fusion(bf16[32,128,256]{2,1,0:T(8,128)(2,1)} %get-tuple-element.307, s32[1024]{0:T(1024)S(1)} %pad_clamp_fusion.5), kind=kCustom, calls=%fused_computation.1.clone.1 | custom fusion | bytes 16777728 | tf_op jit(solution)/shard_map/while/body/jit(_take)/gather | solution.py:22
  305.0 12.9 %convolution_bitcast_fusion.5 = f32[128,128,256]{1,2,0:T(8,128)} fusion(bf16[128,128,128]{2,1,0:T(8,128)(2,1)} %get-tuple-element.308, bf16[128,128,256]{2,1,0:T(8,128)(2,1)} %gather_fusion.1, pred[128]{0:T(512)(128)(4,1)S(1)} %get-tuple-element.249), kind=kOutput, calls=%fused_computation.19.clone.1 | convolution fusion | flops 1077936128 | bytes 29360256 | tf_op jit(solution)/shard_map/while/body/trc,trh->tch/dot_general | solution.py:24
  317.9 17.6 %copy.31 = f32[128,128,256]{0,2,1:T(8,128)} copy(f32[128,128,256]{1,2,0:T(8,128)} %convolution_bitcast_fusion.5) | data formatting | bytes 33554432 | tf_op jit(solution)/shard_map/while/body/trc,trh->tch/dot_general | solution.py:24
  335.5 11.3 %bitcast_select_fusion.5 = f32[128,32768]{0,1:T(8,128)} fusion(f32[128,128,256]{0,2,1:T(8,128)} %copy.31, pred[128]{0:T(512)(128)(4,1)S(1)} %get-tuple-element.250), kind=kLoop, calls=%fused_computation.18.clone.1 | loop fusion | flops 4194304 | bytes 33554560 | tf_op jit(solution)/shard_map/while/body/jit(_where)/select_n | solution.py:33
  346.8 17.4 %copy.32 = f32[128,32768]{1,0:T(8,128)} copy(f32[128,32768]{0,1:T(8,128)} %bitcast_select_fusion.5) | data formatting | bytes 33554432 | tf_op jit(solution)/shard_map/while/body/jit(_where)/select_n | solution.py:33
  364.3 24.3 %scatter_fusion.1 = f32[16,32768]{1,0:T(8,128)S(1)} fusion(f32[16,32768]{1,0:T(8,128)S(1)} %get-tuple-element.292, s32[128]{0:T(128)S(1)} %get-tuple-element.247, f32[128,32768]{1,0:T(8,128)} %copy.32), kind=kCustom, calls=%fused_computation.3.clone.1 | custom fusion | flops 4194304 | bytes 50332160 | tf_op jit(solution)/shard_map/while/body/scatter-add | solution.py:34
  388.8 1.5 reshape.113
  391.0 1.7 multiply_convert_fusion.3
  392.7 29.9 %reduce-scatter.2.cloned.1.call-done = f32[256,256]{1,0:T(8,128)} async-done(((f32[2048,256]{1,0:T(8,128)}), f32[256,256]{1,0:T(8,128)}) %reduce-scatter.2.cloned.1.call-update) | async-done | bytes 262160 | tf_op jit(solution)/shard_map/reduce_scatter | solution.py:79
  422.5 1.7 multiply_convert_fusion.2
  424.2 85.8 %all-reduce.8.cloned.1.call-done = f32[256,256]{1,0:T(8,128)} async-done(((f32[256,256]{1,0:T(8,128)}), f32[256,256]{1,0:T(8,128)}) %all-reduce.8.cloned.1.call-update) | async-done | bytes 262160 | tf_op jit(solution)/shard_map/psum | solution.py:75
  510.0 1.7 copy.52
  (33 shorter events, 3.6 us)
Async XLA Ops:
  7.2 280.5 %copy-start = (bf16[256,256]{1,0:T(8,128)(2,1)S(1)}, bf16[256,256]{1,0:T(8,128)(2,1)}, u32[]{:S(2)}) copy-start(bf16[256,256]{1,0:T(8,128)(2,1)} %param.18) | copy-start | bytes 393220
  7.2 30.3 %all-gather.3.cloned.1.call-start = ((), (), s32[]{:S(2)}) async-start(), calls=%async_computation.1 | async-start | bytes 1179648 | tf_op jit(solution)/shard_map/all_gather | solution.py:51
  8.0 0.6 copy-start.4
  10.3 231.9 %all-reduce.4.cloned.1.call-start = ((), (), s32[]{:S(2)}) async-start(), calls=%async_computation.2 | async-start | bytes 8388608 | tf_op jit(solution)/shard_map/psum | solution.py:59
  37.5 2.3 copy-start.2
  139.5 0.8 copy-start.3
  139.5 148.1 %all-gather.5.cloned.1.call-start = ((), (), s32[]{:S(2)}) async-start(), calls=%async_computation.3 | async-start | bytes 2228224 | tf_op jit(solution)/shard_map/all_gather | solution.py:62
  140.3 250.2 %all-reduce.6.cloned.1.call-start = ((), (), s32[]{:S(2)}) async-start(), calls=%async_computation.5 | async-start | bytes 524288 | tf_op jit(solution)/shard_map/psum | solution.py:75
  295.8 126.7 %reduce-scatter.2.cloned.1.call-start = ((), (), s32[]{:S(2)}) async-start(), calls=%async_computation.4 | async-start | bytes 2359296 | tf_op jit(solution)/shard_map/reduce_scatter | solution.py:79
  388.8 33.7 %copy-start.5 = (f32[256]{0:T(256)S(1)}, f32[256]{0:T(256)}, u32[]{:S(2)}) copy-start(f32[256]{0:T(256)} %copy-done.4) | copy-start | bytes 3076
  388.8 122.9 %copy-start.1 = (bf16[256,256]{1,0:T(8,128)(2,1)S(1)}, bf16[256,256]{1,0:T(8,128)(2,1)}, u32[]{:S(2)}) copy-start(bf16[256,256]{1,0:T(8,128)(2,1)} %param.18) | copy-start | bytes 393220
  390.4 119.6 %all-reduce.8.cloned.1.call-start = ((), (), s32[]{:S(2)}) async-start(), calls=%async_computation.6 | async-start | bytes 524288 | tf_op jit(solution)/shard_map/psum | solution.py:75
Sparse Core Ops, SparseCore 0:
  10.4 27.0 all-gather.2
  139.7 102.4 all-reduce.3
  244.3 43.3 all-gather.4
  295.9 59.3 all-reduce.5
  390.5 31.9 reduce-scatter.1
  425.5 84.4 all-reduce.7
